TPU v7x, 32 devices: a whole 2x2x4 slice. The times are simulated.
32 devices in a mesh: term: 4 (over y, x), sector: 8 (over z, core).
Axes of the slice: x: 2, y: 2, z: 4, core: 2. Of those that a mesh axis runs over, the one named last changes fastest.
Arguments:
- psi: bfloat16 [8, 8, 128, 128], P('sector'), may hold values from -6 to 6
- left_env: bfloat16 [8, 8, 128, 128], P('term', 'sector'), may hold values from -40 to 40
- right_env: bfloat16 [8, 8, 128, 128], P('term', 'sector'), may hold values from -4 to 4
- precond: bfloat16 [8, 8, 128, 128], P('sector'), may hold values from 0.5 to 4
- block_sizes: int32 [8], replicated, may hold values from 32 to 128, as said below
Outputs:
- state: bfloat16 [8, 8, 128, 128], P('sector')
- energy: float32 [3], replicated
Inputs may be any that keep to these rules, and one draw needn't show every extreme that they name: `block_sizes`: some sector has exactly 128 rows in every draw.
All inputs are finite; a program needn't handle non-finite values.
Results may differ from a plain program's by a relative error of at most 0.022.
Values may be sent and summed in bfloat16 or wider, within the bound.
No kernel may reach another device: no remote copies, remote signals or barrier semaphores. Data moves between devices by JAX's collectives and lax.ppermute only.
A program may use at most 128 MiB of HBM per device.

v0:
```python
import jax
import jax.numpy as jnp
from jax import lax
from jax.sharding import PartitionSpec as P

ITERS = 3


def block_mask(block_sizes, width, own_row):
    rows = jnp.arange(width)
    valid = rows[None, :] < block_sizes[:, None]
    own_valid = lax.dynamic_slice_in_dim(valid, own_row, 1, 0)[0]
    return (own_valid[None, :, None] & valid[:, None, :]).astype(jnp.float32)


def dot_sums(cur_share, img_share, pre_share, count):
    first = lax.psum(
        (jnp.sum(cur_share * cur_share), jnp.sum(cur_share * img_share)), ("term", "sector")
    )
    theta = first[1] / first[0]
    fresh = cur_share - (img_share - theta * cur_share) / pre_share
    squares = lax.psum(jnp.sum(fresh * fresh), ("term", "sector"))
    return (theta, lax.rsqrt(squares / count + 1e-06))


def local(psi, left_env, right_env, precond, block_sizes):
    sectors = block_sizes.shape[0]
    width = psi.shape[-1]
    own_row = lax.axis_index("sector")
    share = sectors // lax.axis_size("term")
    share_start = lax.axis_index("term") * share
    count = float(sectors * sectors * width * width)
    mask = block_mask(block_sizes, width, own_row)
    state = (psi[0].astype(jnp.float32) * mask).astype(jnp.bfloat16)
    scaling = precond[0].astype(jnp.float32)
    left_own = left_env[:, 0]

    def portion(values):
        return lax.dynamic_slice_in_dim(values, share_start, share, 0)

    right_all = lax.all_gather(right_env, "sector", axis=1, tiled=True)
    energies = []
    for step in range(ITERS):
        images = jnp.einsum(
            "jab,kjcb->kjac", state, right_all, preferred_element_type=jnp.float32
        ).astype(jnp.bfloat16)
        partial_value = jnp.einsum(
            "kac,kjcd->jad", left_own, images, preferred_element_type=jnp.float32
        )
        current = state.astype(jnp.float32)
        image = lax.psum(partial_value.astype(jnp.bfloat16), "term").astype(jnp.float32) * mask
        theta, factor = dot_sums(portion(current), portion(image), portion(scaling), count)
        fresh = current - (image - theta * current) / scaling
        state = (fresh * factor).astype(jnp.bfloat16)
        energies.append(theta)
    return (state[None], jnp.stack(energies))


def solution(mesh):
    in_specs = (
        P("sector", None, None, None),
        P("term", "sector", None, None),
        P("term", "sector", None, None),
        P("sector", None, None, None),
        P(),
    )
    out_specs = (P("sector", None, None, None), P())
    return jax.shard_map(local, mesh=mesh, in_specs=in_specs, out_specs=out_specs, check_vma=False)
```

profile of v0, /device:TPU:0, one launch (start us, length us, event | category | flops | bytes accessed | tf_op | source)
XLA Modules:
  0.0 424.9 jit_solution(16946019127858269423)
XLA Ops:
  7.2 0.6 copy-done.6
  7.9 0.1 iota_compare_fusion
  8.0 1.1 copy.7
  9.1 16.6 %all_gather.3 = bf16[2,8,128,128]{3,2,1,0:T(8,128)(2,1)S(1)} all-gather(bf16[2,1,128,128]{3,2,1,0:T(8,128)(2,1)S(1)} %copy-done.5), channel_id=1, replica_groups=mesh['term'=4,'sector'=8] {'sector'}, dimensions={1}, use_global_device_ids=true | all-gather | bytes 589824 | tf_op jit(solution)/shard_map/all_gather | solution.py:41
  25.7 1.2 fusion.8
  27.1 0.9 copy-done.4
  27.9 0.2 copy.8
  28.1 43.0 %all-reduce.7.cloned.1.call-done = bf16[8,128,128]{1,2,0:T(8,128)(2,1)} async-done(((bf16[8,128,128]{1,2,0:T(8,128)(2,1)}), bf16[8,128,128]{1,2,0:T(8,128)(2,1)}) %all-reduce.7.cloned.1.call-update) | async-done | bytes 262160 | tf_op jit(solution)/shard_map/psum | solution.py:51
  71.1 1.2 fusion.34
  72.3 0.6 multiply_reduce_fusion.4
  72.9 39.6 %all-reduce.2 = (f32[]{:T(128)}, f32[]{:T(128)}) all-reduce(f32[]{:T(128)} %get-tuple-element.9, f32[]{:T(128)} %get-tuple-element.8), channel_id=1, replica_groups=mesh['term'=4,'sector'=8] {'term','sector'}, use_global_device_ids=true, to_apply=%region_2.0 | all-reduce | flops 2 | bytes 16 | tf_op jit(solution)/shard_map/psum | solution.py:17
  113.9 0.7 fusion.43
  114.5 41.4 %psum.87 = f32[]{:T(128)} all-reduce(f32[]{:T(128)} %fusion.43), channel_id=1, replica_groups=mesh['term'=4,'sector'=8] {'term','sector'}, use_global_device_ids=true, to_apply=%region_6.0 | all-reduce | flops 1 | bytes 8 | tf_op jit(solution)/shard_map/psum | solution.py:22
  156.6 0.3 fusion.52
  156.9 1.2 fusion.7
  158.1 43.0 %all-reduce.9.cloned.1.call-done = bf16[8,128,128]{1,2,0:T(8,128)(2,1)} async-done(((bf16[8,128,128]{1,2,0:T(8,128)(2,1)}), bf16[8,128,128]{1,2,0:T(8,128)(2,1)}) %all-reduce.9.cloned.1.call-update) | async-done | bytes 262160 | tf_op jit(solution)/shard_map/psum | solution.py:51
  201.2 1.1 and_select_fusion.1
  202.3 0.6 multiply_reduce_fusion.2
  203.0 39.6 %all-reduce.1 = (f32[]{:T(128)}, f32[]{:T(128)}) all-reduce(f32[]{:T(128)} %get-tuple-element.7, f32[]{:T(128)} %get-tuple-element.6), channel_id=1, replica_groups=mesh['term'=4,'sector'=8] {'term','sector'}, use_global_device_ids=true, to_apply=%region_9.0 | all-reduce | flops 2 | bytes 16 | tf_op jit(solution)/shard_map/psum | solution.py:17
  243.9 0.7 fusion.42
  244.5 41.4 %psum.91 = f32[]{:T(128)} all-reduce(f32[]{:T(128)} %fusion.42), channel_id=1, replica_groups=mesh['term'=4,'sector'=8] {'term','sector'}, use_global_device_ids=true, to_apply=%region_13.0 | all-reduce | flops 1 | bytes 8 | tf_op jit(solution)/shard_map/psum | solution.py:22
  286.6 0.3 fusion.50
  286.9 1.2 fusion.6
  288.1 43.1 %all-reduce.11.cloned.1.call-done = bf16[8,128,128]{1,2,0:T(8,128)(2,1)} async-done(((bf16[8,128,128]{1,2,0:T(8,128)(2,1)}), bf16[8,128,128]{1,2,0:T(8,128)(2,1)}) %all-reduce.11.cloned.1.call-update) | async-done | bytes 262160 | tf_op jit(solution)/shard_map/psum | solution.py:51
  331.2 1.1 and_select_fusion
  332.3 0.6 multiply_reduce_fusion
  333.0 39.6 %all-reduce = (f32[]{:T(128)}, f32[]{:T(128)}) all-reduce(f32[]{:T(128)} %get-tuple-element.5, f32[]{:T(128)} %get-tuple-element.4), channel_id=1, replica_groups=mesh['term'=4,'sector'=8] {'term','sector'}, use_global_device_ids=true, to_apply=%region_16.0 | all-reduce | flops 2 | bytes 16 | tf_op jit(solution)/shard_map/psum | solution.py:17
  373.9 0.7 fusion.41
  374.5 41.4 %psum.95 = f32[]{:T(128)} all-reduce(f32[]{:T(128)} %fusion.41), channel_id=1, replica_groups=mesh['term'=4,'sector'=8] {'term','sector'}, use_global_device_ids=true, to_apply=%region_20.0 | all-reduce | flops 1 | bytes 8 | tf_op jit(solution)/shard_map/psum | solution.py:22
  416.6 0.3 fusion.31
  416.9 0.9 copy.9
  417.7 0.6 pad_maximum_fusion
  (20 shorter events, 0.2 us)
Async XLA Ops:
  7.2 18.6 %copy-start = (bf16[2,1,128,128]{3,2,1,0:T(8,128)(2,1)S(1)}, bf16[2,1,128,128]{3,2,1,0:T(8,128)(2,1)}, u32[]{:S(2)}) copy-start(bf16[2,1,128,128]{3,2,1,0:T(8,128)(2,1)} %param.6) | copy-start | bytes 196612
  7.2 64.0 %all-reduce.7.cloned.1.call-start = ((), (), s32[]{:S(2)}) async-start(), calls=%async_computation | async-start | bytes 524288 | tf_op jit(solution)/shard_map/psum | solution.py:51
  7.2 0.7 copy-start.6
  8.0 1.2 copy-start.5
  27.0 0.9 copy-start.4
  27.0 174.2 %all-reduce.9.cloned.1.call-start = ((), (), s32[]{:S(2)}) async-start(), calls=%async_computation.1 | async-start | bytes 524288 | tf_op jit(solution)/shard_map/psum | solution.py:51
  72.9 83.6 %copy-start.1 = (bf16[8,128,128]{1,2,0:T(8,128)(2,1)S(1)}, bf16[8,128,128]{1,2,0:T(8,128)(2,1)}, u32[]{:S(2)}) copy-start(bf16[8,128,128]{1,2,0:T(8,128)(2,1)} %all-reduce.7.cloned.1.call-done) | copy-start | bytes 786436
  158.1 173.1 %all-reduce.11.cloned.1.call-start = ((), (), s32[]{:S(2)}) async-start(), calls=%async_computation.2 | async-start | bytes 524288 | tf_op jit(solution)/shard_map/psum | solution.py:51
  203.0 83.6 %copy-start.3 = (bf16[8,128,128]{1,2,0:T(8,128)(2,1)S(1)}, bf16[8,128,128]{1,2,0:T(8,128)(2,1)}, u32[]{:S(2)}) copy-start(bf16[8,128,128]{1,2,0:T(8,128)(2,1)} %all-reduce.9.cloned.1.call-done) | copy-start | bytes 786436
  333.0 83.6 %copy-start.2 = (bf16[8,128,128]{1,2,0:T(8,128)(2,1)S(1)}, bf16[8,128,128]{1,2,0:T(8,128)(2,1)}, u32[]{:S(2)}) copy-start(bf16[8,128,128]{1,2,0:T(8,128)(2,1)} %all-reduce.11.cloned.1.call-done) | copy-start | bytes 786436
Sparse Core Ops, SparseCore 0:
  27.1 43.9 all-reduce.6
  158.2 42.9 all-reduce.8
  288.2 42.9 all-reduce.10
where the time goes:
time: 426 us; the launch traced here: 425 us
  blocking collectives  259 us (61%)
  waiting for transfers between devices  129 us (30%)
  between operations  20 us (5%)
  other arithmetic  8.96 us (2%)
    psum x3, waiting for transfers between devices, local(): lax.psum(partial_value.astype(jnp.bfloat16), 'term').astype(jnp.float32)  129 us
    psum x3, blocking collectives, dot_sums(): squares = lax.psum(jnp.sum(fresh * fresh), ('term', 'sector'))  124 us
    psum x3, blocking collectives, dot_sums(): lax.psum((jnp.sum(cur_share * cur_share), jnp.sum(cur_share * img_share))...  119 us
    all_gather x1, blocking collectives, local(): right_all = lax.all_gather(right_env, 'sector', axis=1, tiled=True)  16.6 us
  transfers between devices with their start and end apart: 3, of which 3 were waited for; matrix products, arithmetic and copies ran while one was open for 0% of the time, Pallas kernels for 0%

commit v1 on v0

--- a/solution.py
+++ b/solution.py
@@ -38,7 +38,14 @@
     def portion(values):
         return lax.dynamic_slice_in_dim(values, share_start, share, 0)
 
-    right_all = lax.all_gather(right_env, "sector", axis=1, tiled=True)
+    ring = [right_env]
+    for hop in range(7):
+        ring.append(lax.ppermute(ring[-1], "sector", [(dev, (dev + 1) % 8) for dev in range(8)]))
+    right_all = jnp.roll(
+        jnp.concatenate(ring[::-1], axis=1),
+        (lax.axis_index("sector") + 1) * ring[0].shape[1],
+        axis=1,
+    )
     energies = []
     for step in range(ITERS):
         images = jnp.einsum(

time: 426 us -> 446 us (1.047)
  waiting for transfers between devices: 129 us -> 164 us
  blocking collectives: 259 us -> 243 us
    ppermute x0 -> x7, waiting for transfers between devices: none -> 37.2 us  [local(): lax.ppermute(ring[-1], 'sector', [(dev, (dev + 1) % 8) for dev in range(8)])]
    all_gather x1 -> x0, blocking collectives: 16.6 us -> none  [local(): right_all = lax.all_gather(right_env, 'sector', axis=1, tiled=True)]
  transfers between devices with their start and end apart: 3 -> 10, of which waited for: 3 -> 10; matrix products, arithmetic and copies ran while one was open for 0% -> 0% of each run, Pallas kernels for 0% -> 0%
where the time goes in v1:
time: 446 us; the launch traced here: 445 us
  blocking collectives  243 us (54%)
  waiting for transfers between devices  164 us (37%)
  between operations  20 us (4%)
  other arithmetic  9.61 us (2%)
    psum x3, waiting for transfers between devices, local(): lax.psum(partial_value.astype(jnp.bfloat16), 'term').astype(jnp.float32)  127 us
    psum x3, blocking collectives, dot_sums(): squares = lax.psum(jnp.sum(fresh * fresh), ('term', 'sector'))  124 us
    psum x3, blocking collectives, dot_sums(): lax.psum((jnp.sum(cur_share * cur_share), jnp.sum(cur_share * img_share))...  119 us
    ppermute x7, waiting for transfers between devices, local(): lax.ppermute(ring[-1], 'sector', [(dev, (dev + 1) % 8) for dev in range(8)])  37.2 us
  transfers between devices with their start and end apart: 10, of which 10 were waited for; matrix products, arithmetic and copies ran while one was open for 0% of the time, Pallas kernels for 0%

profile of v1, /device:TPU:0, one launch (start us, length us, event | category | flops | bytes accessed | tf_op | source)
XLA Modules:
  0.0 444.9 jit_solution(5949829578810973409)
XLA Ops:
  7.7 6.2 %collective-permute-done = bf16[2,1,128,128]{3,2,1,0:T(8,128)(2,1)S(1)} collective-permute-done((bf16[2,1,128,128]{3,2,1,0:T(8,128)(2,1)}, bf16[2,1,128,128]{3,2,1,0:T(8,128)(2,1)S(1)}, u32[]{:S(2)}, u32[]{:S(2)}) %collective-permute-start) | collective-permute-done | bytes 65568 | tf_op jit(solution)/shard_map/ppermute | solution.py:43
  13.9 5.5 %collective-permute-done.1 = bf16[2,1,128,128]{3,2,1,0:T(8,128)(2,1)S(1)} collective-permute-done((bf16[2,1,128,128]{3,2,1,0:T(8,128)(2,1)S(1)}, bf16[2,1,128,128]{3,2,1,0:T(8,128)(2,1)S(1)}, u32[]{:S(2)}, u32[]{:S(2)}) %collective-permute-start.1) | collective-permute-done | bytes 65568 | tf_op jit(solution)/shard_map/ppermute | solution.py:43
  19.4 5.5 %collective-permute-done.2 = bf16[2,1,128,128]{3,2,1,0:T(8,128)(2,1)S(1)} collective-permute-done((bf16[2,1,128,128]{3,2,1,0:T(8,128)(2,1)S(1)}, bf16[2,1,128,128]{3,2,1,0:T(8,128)(2,1)S(1)}, u32[]{:S(2)}, u32[]{:S(2)}) %collective-permute-start.2) | collective-permute-done | bytes 65568 | tf_op jit(solution)/shard_map/ppermute | solution.py:43
  24.9 5.5 %collective-permute-done.3 = bf16[2,1,128,128]{3,2,1,0:T(8,128)(2,1)S(1)} collective-permute-done((bf16[2,1,128,128]{3,2,1,0:T(8,128)(2,1)S(1)}, bf16[2,1,128,128]{3,2,1,0:T(8,128)(2,1)S(1)}, u32[]{:S(2)}, u32[]{:S(2)}) %collective-permute-start.3) | collective-permute-done | bytes 65568 | tf_op jit(solution)/shard_map/ppermute | solution.py:43
  30.4 5.5 %collective-permute-done.4 = bf16[2,1,128,128]{3,2,1,0:T(8,128)(2,1)S(1)} collective-permute-done((bf16[2,1,128,128]{3,2,1,0:T(8,128)(2,1)S(1)}, bf16[2,1,128,128]{3,2,1,0:T(8,128)(2,1)S(1)}, u32[]{:S(2)}, u32[]{:S(2)}) %collective-permute-start.4) | collective-permute-done | bytes 65568 | tf_op jit(solution)/shard_map/ppermute | solution.py:43
  35.9 0.7 iota_compare_fusion
  36.6 1.1 copy.7
  37.7 3.6 collective-permute-done.5
  41.4 5.5 %collective-permute-done.6 = bf16[2,1,128,128]{3,2,1,0:T(8,128)(2,1)S(1)} collective-permute-done((bf16[2,1,128,128]{3,2,1,0:T(8,128)(2,1)S(1)}, bf16[2,1,128,128]{3,2,1,0:T(8,128)(2,1)S(1)}, u32[]{:S(2)}, u32[]{:S(2)}) %collective-permute-start.6) | collective-permute-done | bytes 65568 | tf_op jit(solution)/shard_map/ppermute | solution.py:43
  47.0 0.8 copy-done.5
  48.0 1.3 fusion.8
  49.4 0.9 copy-done.4
  50.5 40.7 %all-reduce.7.cloned.1.call-done = bf16[8,128,128]{1,2,0:T(8,128)(2,1)} async-done(((bf16[8,128,128]{1,2,0:T(8,128)(2,1)}), bf16[8,128,128]{1,2,0:T(8,128)(2,1)}) %all-reduce.7.cloned.1.call-update) | async-done | bytes 262160 | tf_op jit(solution)/shard_map/psum | solution.py:58
  91.2 1.2 fusion.34
  93.0 39.6 %all-reduce.2 = (f32[]{:T(128)}, f32[]{:T(128)}) all-reduce(f32[]{:T(128)} %get-tuple-element.9, f32[]{:T(128)} %get-tuple-element.8), channel_id=1, replica_groups=mesh['term'=4,'sector'=8] {'term','sector'}, use_global_device_ids=true, to_apply=%region_2.3 | all-reduce | flops 2 | bytes 16 | tf_op jit(solution)/shard_map/psum | solution.py:17
  133.9 0.7 fusion.43
  134.5 41.4 %psum.87 = f32[]{:T(128)} all-reduce(f32[]{:T(128)} %fusion.43), channel_id=1, replica_groups=mesh['term'=4,'sector'=8] {'term','sector'}, use_global_device_ids=true, to_apply=%region_6.7 | all-reduce | flops 1 | bytes 8 | tf_op jit(solution)/shard_map/psum | solution.py:22
  176.9 1.2 fusion.7
  178.2 43.0 %all-reduce.9.cloned.1.call-done = bf16[8,128,128]{1,2,0:T(8,128)(2,1)} async-done(((bf16[8,128,128]{1,2,0:T(8,128)(2,1)}), bf16[8,128,128]{1,2,0:T(8,128)(2,1)}) %all-reduce.9.cloned.1.call-update) | async-done | bytes 262160 | tf_op jit(solution)/shard_map/psum | solution.py:58
  221.2 1.1 and_select_fusion.1
  222.3 0.6 multiply_reduce_fusion.2
  223.0 39.6 %all-reduce.1 = (f32[]{:T(128)}, f32[]{:T(128)}) all-reduce(f32[]{:T(128)} %get-tuple-element.7, f32[]{:T(128)} %get-tuple-element.6), channel_id=1, replica_groups=mesh['term'=4,'sector'=8] {'term','sector'}, use_global_device_ids=true, to_apply=%region_9.10 | all-reduce | flops 2 | bytes 16 | tf_op jit(solution)/shard_map/psum | solution.py:17
  263.9 0.7 fusion.42
  264.5 41.4 %psum.91 = f32[]{:T(128)} all-reduce(f32[]{:T(128)} %fusion.42), channel_id=1, replica_groups=mesh['term'=4,'sector'=8] {'term','sector'}, use_global_device_ids=true, to_apply=%region_13.14 | all-reduce | flops 1 | bytes 8 | tf_op jit(solution)/shard_map/psum | solution.py:22
  306.9 1.2 fusion.6
  308.1 43.1 %all-reduce.11.cloned.1.call-done = bf16[8,128,128]{1,2,0:T(8,128)(2,1)} async-done(((bf16[8,128,128]{1,2,0:T(8,128)(2,1)}), bf16[8,128,128]{1,2,0:T(8,128)(2,1)}) %all-reduce.11.cloned.1.call-update) | async-done | bytes 262160 | tf_op jit(solution)/shard_map/psum | solution.py:58
  351.2 1.1 and_select_fusion
  352.4 0.6 multiply_reduce_fusion
  353.0 39.6 %all-reduce = (f32[]{:T(128)}, f32[]{:T(128)}) all-reduce(f32[]{:T(128)} %get-tuple-element.5, f32[]{:T(128)} %get-tuple-element.4), channel_id=1, replica_groups=mesh['term'=4,'sector'=8] {'term','sector'}, use_global_device_ids=true, to_apply=%region_16.17 | all-reduce | flops 2 | bytes 16 | tf_op jit(solution)/shard_map/psum | solution.py:17
  393.9 0.7 fusion.41
  394.6 41.4 %psum.95 = f32[]{:T(128)} all-reduce(f32[]{:T(128)} %fusion.41), channel_id=1, replica_groups=mesh['term'=4,'sector'=8] {'term','sector'}, use_global_device_ids=true, to_apply=%region_20.21 | all-reduce | flops 1 | bytes 8 | tf_op jit(solution)/shard_map/psum | solution.py:22
  436.9 0.9 copy.9
  (48 shorter events, 3.4 us)
Async XLA Ops:
  7.2 40.9 %copy-start = (bf16[2,1,128,128]{3,2,1,0:T(8,128)(2,1)S(1)}, bf16[2,1,128,128]{3,2,1,0:T(8,128)(2,1)}, u32[]{:S(2)}) copy-start(bf16[2,1,128,128]{3,2,1,0:T(8,128)(2,1)} %param.6) | copy-start | bytes 196612
  7.2 84.0 %all-reduce.7.cloned.1.call-start = ((), (), s32[]{:S(2)}) async-start(), calls=%async_computation | async-start | bytes 524288 | tf_op jit(solution)/shard_map/psum | solution.py:58
  7.2 6.7 %collective-permute-start = (bf16[2,1,128,128]{3,2,1,0:T(8,128)(2,1)}, bf16[2,1,128,128]{3,2,1,0:T(8,128)(2,1)S(1)}, u32[]{:S(2)}, u32[]{:S(2)}) collective-permute-start(bf16[2,1,128,128]{3,2,1,0:T(8,128)(2,1)} %param.7), channel_id=1, source_target_pairs={{0,1},{1,2},{2,3},{3,4},{4,5},{5,6},{6,7},{7,0},{8,9},{9,10},{10,1... | collective-permute-start | bytes 196616 | tf_op jit(solution)/shard_map/ppermute | solution.py:43
  13.9 5.5 %collective-permute-start.1 = (bf16[2,1,128,128]{3,2,1,0:T(8,128)(2,1)S(1)}, bf16[2,1,128,128]{3,2,1,0:T(8,128)(2,1)S(1)}, u32[]{:S(2)}, u32[]{:S(2)}) collective-permute-start(bf16[2,1,128,128]{3,2,1,0:T(8,128)(2,1)S(1)} %collective-permute-done), channel_id=1, source_target_pairs={{0,1},{1,2},{2,3},{3,4},{4,5},{5,6},{6,7},{7,0},{8,9},{9,10},{10,1... | collective-permute-start | bytes 196616 | tf_op jit(solution)/shard_map/ppermute | solution.py:43
  19.4 5.5 %collective-permute-start.2 = (bf16[2,1,128,128]{3,2,1,0:T(8,128)(2,1)S(1)}, bf16[2,1,128,128]{3,2,1,0:T(8,128)(2,1)S(1)}, u32[]{:S(2)}, u32[]{:S(2)}) collective-permute-start(bf16[2,1,128,128]{3,2,1,0:T(8,128)(2,1)S(1)} %collective-permute-done.1), channel_id=1, source_target_pairs={{0,1},{1,2},{2,3},{3,4},{4,5},{5,6},{6,7},{7,0},{8,9},{9,10},{10,1... | collective-permute-start | bytes 196616 | tf_op jit(solution)/shard_map/ppermute | solution.py:43
  24.9 5.5 %collective-permute-start.3 = (bf16[2,1,128,128]{3,2,1,0:T(8,128)(2,1)S(1)}, bf16[2,1,128,128]{3,2,1,0:T(8,128)(2,1)S(1)}, u32[]{:S(2)}, u32[]{:S(2)}) collective-permute-start(bf16[2,1,128,128]{3,2,1,0:T(8,128)(2,1)S(1)} %collective-permute-done.2), channel_id=1, source_target_pairs={{0,1},{1,2},{2,3},{3,4},{4,5},{5,6},{6,7},{7,0},{8,9},{9,10},{10,1... | collective-permute-start | bytes 196616 | tf_op jit(solution)/shard_map/ppermute | solution.py:43
  30.4 5.5 %collective-permute-start.4 = (bf16[2,1,128,128]{3,2,1,0:T(8,128)(2,1)S(1)}, bf16[2,1,128,128]{3,2,1,0:T(8,128)(2,1)S(1)}, u32[]{:S(2)}, u32[]{:S(2)}) collective-permute-start(bf16[2,1,128,128]{3,2,1,0:T(8,128)(2,1)S(1)} %collective-permute-done.3), channel_id=1, source_target_pairs={{0,1},{1,2},{2,3},{3,4},{4,5},{5,6},{6,7},{7,0},{8,9},{9,10},{10,1... | collective-permute-start | bytes 196616 | tf_op jit(solution)/shard_map/ppermute | solution.py:43
  35.9 5.5 %collective-permute-start.5 = (bf16[2,1,128,128]{3,2,1,0:T(8,128)(2,1)S(1)}, bf16[2,1,128,128]{3,2,1,0:T(8,128)(2,1)S(1)}, u32[]{:S(2)}, u32[]{:S(2)}) collective-permute-start(bf16[2,1,128,128]{3,2,1,0:T(8,128)(2,1)S(1)} %collective-permute-done.4), channel_id=1, source_target_pairs={{0,1},{1,2},{2,3},{3,4},{4,5},{5,6},{6,7},{7,0},{8,9},{9,10},{10,1... | collective-permute-start | bytes 196616 | tf_op jit(solution)/shard_map/ppermute | solution.py:43
  41.4 5.5 %collective-permute-start.6 = (bf16[2,1,128,128]{3,2,1,0:T(8,128)(2,1)S(1)}, bf16[2,1,128,128]{3,2,1,0:T(8,128)(2,1)S(1)}, u32[]{:S(2)}, u32[]{:S(2)}) collective-permute-start(bf16[2,1,128,128]{3,2,1,0:T(8,128)(2,1)S(1)} %collective-permute-done.5), channel_id=1, source_target_pairs={{0,1},{1,2},{2,3},{3,4},{4,5},{5,6},{6,7},{7,0},{8,9},{9,10},{10,1... | collective-permute-start | bytes 196616 | tf_op jit(solution)/shard_map/ppermute | solution.py:43
  47.0 0.8 copy-start.5
  49.3 0.9 copy-start.4
  49.3 171.8 %all-reduce.9.cloned.1.call-start = ((), (), s32[]{:S(2)}) async-start(), calls=%async_computation.1 | async-start | bytes 524288 | tf_op jit(solution)/shard_map/psum | solution.py:58
  93.0 83.6 %copy-start.1 = (bf16[8,128,128]{1,2,0:T(8,128)(2,1)S(1)}, bf16[8,128,128]{1,2,0:T(8,128)(2,1)}, u32[]{:S(2)}) copy-start(bf16[8,128,128]{1,2,0:T(8,128)(2,1)} %all-reduce.7.cloned.1.call-done) | copy-start | bytes 786436
  178.1 173.1 %all-reduce.11.cloned.1.call-start = ((), (), s32[]{:S(2)}) async-start(), calls=%async_computation.2 | async-start | bytes 524288 | tf_op jit(solution)/shard_map/psum | solution.py:58
  223.0 83.6 %copy-start.3 = (bf16[8,128,128]{1,2,0:T(8,128)(2,1)S(1)}, bf16[8,128,128]{1,2,0:T(8,128)(2,1)}, u32[]{:S(2)}) copy-start(bf16[8,128,128]{1,2,0:T(8,128)(2,1)} %all-reduce.9.cloned.1.call-done) | copy-start | bytes 786436
  353.0 83.6 %copy-start.2 = (bf16[8,128,128]{1,2,0:T(8,128)(2,1)S(1)}, bf16[8,128,128]{1,2,0:T(8,128)(2,1)}, u32[]{:S(2)}) copy-start(bf16[8,128,128]{1,2,0:T(8,128)(2,1)} %all-reduce.11.cloned.1.call-done) | copy-start | bytes 786436
Sparse Core Ops, SparseCore 0:
  49.5 41.6 all-reduce.6
  178.2 42.8 all-reduce.8
  308.3 42.9 all-reduce.10
